TPU v7x, 512 devices: a whole 4x4x16 slice. The times are simulated.
512 devices in a mesh: dp: 8 (over y, core), expert: 64 (over x, z).
Axes of the slice: x: 4, y: 4, z: 16, core: 2. Of those that a mesh axis runs over, the one named last changes fastest.
Arguments:
- grad_out: bfloat16 [32768, 4096], P('expert', 'dp'), may hold values from -30 to 30
- hidden: bfloat16 [32768, 2, 1024], P('expert', None, 'dp'), may hold values from -24 to 24
- gate_prob: float32 [32768, 2], P('expert'), may hold values from 0.05 to 1
- expert_ids: int32 [32768, 2], P('expert'), may hold values from 0 to 63, all different within a row; in each aligned block of 512 rows (0 to 511, 512 to 1023, ...) at most 20 rows name the same one
- weights: bfloat16 [64, 1024, 4096], P('expert', None, 'dp'), may hold values from -0.1875 to 0.1875
Outputs:
- hidden_grad: bfloat16 [32768, 2, 1024], P('expert', None, 'dp')
- update: float32 [64, 1024, 4096], P('expert', None, 'dp')
Inputs may be any that keep to these rules, and one draw needn't show every extreme that they name: `expert_ids`: among the 512 tokens of one index of expert, no expert is named by more than 20 choices, a bound that some block reaches; the 2 experts of a token differ.
All inputs are finite; a program needn't handle non-finite values.
Results may differ from a plain program's by a relative error of at most 0.019.
Values may be sent and summed in bfloat16 or wider, within the bound.
No kernel may reach another device: no remote copies, remote signals or barrier semaphores. Data moves between devices by JAX's collectives and lax.ppermute only.
A program may use at most 64 MiB of HBM per device.

v0:
```python
import jax
import jax.numpy as jnp
from jax import lax
from jax.sharding import PartitionSpec as P

D = 4096


def slot_numbers(route_ids, capacity, expert_count):
    flat_ids = route_ids.reshape(-1)
    one_hot = (flat_ids[:, None] == jnp.arange(expert_count, dtype=jnp.int32)[None, :]).astype(
        jnp.int32
    )
    before = jnp.cumsum(one_hot, axis=0) - one_hot
    rank_in = jnp.sum(before * one_hot, axis=1)
    return flat_ids * capacity + rank_in


def gram_sum(matrix_part):
    partial_gram = jnp.dot(matrix_part, matrix_part.T, preferred_element_type=jnp.float32)
    return lax.psum(partial_gram.astype(jnp.bfloat16), "dp").astype(jnp.float32)


def place_slots(slot_index, values, slot_count):
    empty_rows = jnp.zeros((slot_count,) + values.shape[1:], values.dtype)
    return empty_rows.at[slot_index].set(values)


def per_device(grad_out, hidden, gate_prob, expert_ids, weights):
    tokens, width_part = grad_out.shape
    top_count = expert_ids.shape[1]
    experts = lax.axis_size("expert")
    capacity = 5 * tokens * top_count // (4 * experts)
    total_slots = experts * capacity
    pair_count = tokens * top_count
    slot_index = slot_numbers(expert_ids, capacity, experts)
    token_of = jnp.arange(pair_count, dtype=jnp.int32) // top_count
    send_grad = place_slots(slot_index, grad_out[token_of], total_slots).reshape(
        experts, capacity, width_part
    )
    scaled_part = (gate_prob[:, :, None] * hidden.astype(jnp.float32)).astype(jnp.bfloat16)
    whole_scaled = lax.all_gather(scaled_part, "dp", axis=2, tiled=True)
    send_scaled = place_slots(
        slot_index, whole_scaled.reshape(pair_count, -1), total_slots
    ).reshape(experts, capacity, -1)
    got_grad, got_scaled = (
        lax.all_to_all(send_grad, "expert", split_axis=0, concat_axis=0, tiled=True),
        lax.all_to_all(send_scaled, "expert", split_axis=0, concat_axis=0, tiled=True),
    )
    got_grad = got_grad.reshape(total_slots, width_part)
    got_scaled = got_scaled.reshape(total_slots, -1)
    weight_part = weights[0]
    gradient = lax.dot_general(
        got_scaled, got_grad, (((0,), (0,)), ((), ())), preferred_element_type=jnp.float32
    )
    back_term = lax.dot_general(
        got_grad, weight_part, (((1,), (1,)), ((), ())), preferred_element_type=jnp.float32
    )
    flat_prob = gate_prob.reshape(-1)
    summed = lax.psum_scatter(
        back_term.astype(jnp.bfloat16), "dp", scatter_dimension=1, tiled=True
    ).astype(jnp.float32)
    returned = lax.all_to_all(
        summed.reshape(experts, capacity, -1).astype(jnp.bfloat16),
        "expert",
        split_axis=0,
        concat_axis=0,
        tiled=True,
    ).astype(jnp.float32)
    picked = returned.reshape(total_slots, -1)[slot_index]
    hidden_grad = (flat_prob[:, None] * picked).astype(jnp.bfloat16).reshape(tokens, top_count, -1)
    grad_bf16 = gradient.astype(jnp.bfloat16)
    gram_first = gram_sum(grad_bf16)
    norm_sq = jnp.sqrt(jnp.sum(gram_first * gram_first)) + 1e-06
    current = (grad_bf16.astype(jnp.float32) * lax.rsqrt(norm_sq)).astype(jnp.bfloat16)
    gram_now = (gram_first / norm_sq).astype(jnp.bfloat16)
    following = current.astype(jnp.float32)
    for sweep_number in range(2):
        if sweep_number > 0:
            gram_now = gram_sum(current).astype(jnp.bfloat16)
        following = 1.5 * current.astype(jnp.float32) - 0.5 * jnp.dot(
            gram_now, current, preferred_element_type=jnp.float32
        )
        current = following.astype(jnp.bfloat16)
    update = following * D**0.5
    return (hidden_grad, update[None])


def solution(mesh):
    in_specs = (
        P("expert", "dp"),
        P("expert", None, "dp"),
        P("expert", None),
        P("expert", None),
        P("expert", None, "dp"),
    )
    out_specs = (P("expert", None, "dp"), P("expert", None, "dp"))
    return jax.shard_map(
        per_device, mesh=mesh, in_specs=in_specs, out_specs=out_specs, check_vma=False
    )
```

profile of v0, /device:TPU:2, one launch (start us, length us, event | category | flops | bytes accessed | tf_op | source)
XLA Modules:
  0.0 626.0 jit_solution(6197987789082699378)
XLA Ops:
  7.2 0.0 reduce-scatter.4.cloned.1.call-start
  7.2 0.8 broadcast_multiply_fusion
  8.0 0.8 copy.19
  8.8 0.2 eq.29
  9.0 0.2 eq.25
  9.2 0.1 copy.18
  9.3 0.2 mul.64
  9.6 18.0 %reduce-window.6 = s32[64,8,128]{2,1,0:T(8,128)S(1)} reduce-window(s32[64,8,128]{2,1,0:T(8,128)S(1)} %fusion.21, s32[]{:T(128)} %constant.16.clone.1), window={size=1x1x128 pad=0_0x0_0x127_0}, to_apply=%region_0.0 | reduce-window | flops 8323072 | bytes 524292 | tf_op jit(solution)/shard_map/reduce-window
  27.6 0.1 slice.12
  27.7 0.1 copy.21
  27.9 0.1 copy.22
  28.0 0.1 broadcast_add_fusion
  28.1 0.1 fusion.20
  28.2 12.8 %scatter_custom_fusion = bf16[1280,512]{1,0:T(8,128)(2,1)S(1)} fusion(s32[1024]{0:T(1024)S(1)} %bitcast.46, bf16[512,512]{1,0:T(8,128)(2,1)} %param.5, s32[1024]{0:T(1024)S(1)} %broadcast_clamp_fusion.1, bf16[]{:T(256)} %constant.13.clone.1), kind=kCustom, calls=%fused_computation.22 | custom fusion | bytes 1311232 | tf_op jit(solution)/shard_map/scatter | solution.py:26
  41.0 1.3 reshape.124
  42.3 94.8 %all_to_all.15 = bf16[64,20,512]{2,1,0:T(8,128)(2,1)S(1)} all-to-all(bf16[64,20,512]{2,1,0:T(8,128)(2,1)} %reshape.124), channel_id=1, replica_groups=mesh['dp'=8,'expert'=64] {'expert'}, dimensions={0} | all-to-all | bytes 2621440 | tf_op jit(solution)/shard_map/all_to_all | solution.py:47
  137.1 1.2 reshape.125
  138.3 4.4 convolution_convert_fusion
  142.7 4.4 copy.25
  147.1 0.0 reduce-scatter.4.cloned.1.call-update
  147.1 35.3 %reduce-scatter.4.cloned.1.call-done = bf16[128,1280]{1,0:T(8,128)(2,1)} async-done(((bf16[1024,1280]{1,0:T(8,128)(2,1)}), bf16[128,1280]{1,0:T(8,128)(2,1)}) %reduce-scatter.4.cloned.1.call-update) | async-done | bytes 327696
  182.4 1.2 copy.26
  183.5 0.8 convert_element_type.61
  184.4 15.8 %all-to-all-start.1 = ((bf16[64,20,128]{2,1,0:T(8,128)(2,1)}), bf16[64,20,128]{2,1,0:T(8,128)(2,1)}, u32[]{:S(2)}, u32[]{:S(2)}) async-start(bf16[64,20,128]{2,1,0:T(8,128)(2,1)} %convert_element_type.61), calls=%async_computation.1 | async-start | bytes 786432 | tf_op jit(solution)/shard_map/all_to_all | solution.py:63
  200.2 0.0 all-gather.2.cloned.1.call-start
  200.3 0.1 copy.17
  200.4 23.1 %all-to-all-done.1 = bf16[64,20,128]{2,1,0:T(8,128)(2,1)} async-done(((bf16[64,20,128]{2,1,0:T(8,128)(2,1)}), bf16[64,20,128]{2,1,0:T(8,128)(2,1)}, u32[]{:S(2)}, u32[]{:S(2)}) %all-to-all-start.1) | async-done | bytes 327712 | tf_op jit(solution)/shard_map/all_to_all | solution.py:63
  223.6 1.1 reshape.131
  224.6 4.0 gather_fusion
  228.7 2.4 multiply_convert_fusion.2
  231.1 0.0 all-gather.2.cloned.1.call-update
  231.1 0.2 all-reduce.3.cloned.1.call-start
  231.4 35.5 %all-gather.2.cloned.1.call-done = bf16[512,2,1024]{2,1,0:T(2,128)(2,1)} async-done(((bf16[512,2,128]{2,1,0:T(2,128)(2,1)}), bf16[512,2,1024]{2,1,0:T(2,128)(2,1)}) %all-gather.2.cloned.1.call-update) | async-done | bytes 2097168 | tf_op jit(solution)/shard_map/all_gather | solution.py:42
  266.8 4.1 reshape.160
  270.9 7.8 %scatter_custom_fusion.1 = bf16[1280,1024]{1,0:T(8,128)(2,1)} fusion(s32[1024]{0:T(1024)S(1)} %bitcast.48, bf16[1024,1024]{1,0:T(8,128)(2,1)} %reshape.160, bf16[]{:T(256)} %constant.13.clone.1), kind=kCustom, calls=%fused_computation.19 | custom fusion | bytes 2621952 | tf_op jit(solution)/shard_map/scatter | solution.py:26
  278.7 5.2 reshape.129
  283.9 159.6 %all_to_all.16 = bf16[64,20,1024]{2,1,0:T(8,128)(2,1)S(1)} all-to-all(bf16[64,20,1024]{2,1,0:T(8,128)(2,1)} %reshape.129), channel_id=1, replica_groups=mesh['dp'=8,'expert'=64] {'expert'}, dimensions={0} | all-to-all | bytes 5242880 | tf_op jit(solution)/shard_map/all_to_all | solution.py:48
  443.5 2.9 bitcast_convert_fusion
  446.4 1.0 copy-done.3
  447.3 2.6 convolution_convert_fusion.2
  450.0 0.3 all-reduce.5.cloned.1.call-start
  450.2 73.4 %all-reduce.3.cloned.1.call-done = bf16[1024,1024]{1,0:T(8,128)(2,1)} async-done(((bf16[1024,1024]{1,0:T(8,128)(2,1)}), bf16[1024,1024]{1,0:T(8,128)(2,1)}) %all-reduce.3.cloned.1.call-update) | async-done | bytes 2097168 | tf_op jit(solution)/shard_map/psum | solution.py:21
  523.6 3.4 fusion
  527.8 2.9 subtract_convert_fusion
  530.8 1.0 copy-done.4
  531.7 2.6 convolution_convert_fusion.1
  534.4 80.9 %all-reduce.5.cloned.1.call-done = bf16[1024,1024]{1,0:T(8,128)(2,1)} async-done(((bf16[1024,1024]{1,0:T(8,128)(2,1)}), bf16[1024,1024]{1,0:T(8,128)(2,1)}) %all-reduce.5.cloned.1.call-update) | async-done | bytes 2097168 | tf_op jit(solution)/shard_map/psum | solution.py:21
  615.2 4.2 multiply_bitcast_fusion
  (19 shorter events, 0.1 us)
Async XLA Ops:
  7.2 131.1 %copy-start = (bf16[1,1024,512]{2,1,0:T(8,128)(2,1)S(1)}, bf16[1,1024,512]{2,1,0:T(8,128)(2,1)}, u32[]{:S(2)}) copy-start(bf16[1,1024,512]{2,1,0:T(8,128)(2,1)} %param.9) | copy-start | bytes 3145732
  7.2 175.2 %reduce-scatter.4.cloned.1.call-start = ((), (), s32[]{:S(2)}) async-start(), calls=%async_computation.7 | async-start | bytes 2949120
  147.1 53.2 %copy-start.2 = (f32[512,2]{0,1:T(2,128)S(1)}, f32[512,2]{0,1:T(2,128)}, u32[]{:S(2)}) copy-start(f32[512,2]{0,1:T(2,128)} %param.7) | copy-start | bytes 12292
  184.4 39.2 %all-to-all-start.1 = ((bf16[64,20,128]{2,1,0:T(8,128)(2,1)}), bf16[64,20,128]{2,1,0:T(8,128)(2,1)}, u32[]{:S(2)}, u32[]{:S(2)}) async-start(bf16[64,20,128]{2,1,0:T(8,128)(2,1)} %convert_element_type.61), calls=%async_computation.1 | async-start | bytes 786432 | tf_op jit(solution)/shard_map/all_to_all | solution.py:63
  200.2 66.6 %all-gather.2.cloned.1.call-start = ((), (), s32[]{:S(2)}) async-start(), calls=%async_computation.4 | async-start | bytes 2359296 | tf_op jit(solution)/shard_map/all_gather | solution.py:42
  231.1 292.5 %all-reduce.3.cloned.1.call-start = ((), (), s32[]{:S(2)}) async-start(), calls=%async_computation.5 | async-start | bytes 4194304 | tf_op jit(solution)/shard_map/psum | solution.py:21
  446.4 1.0 copy-start.3
  450.0 165.3 %all-reduce.5.cloned.1.call-start = ((), (), s32[]{:S(2)}) async-start(), calls=%async_computation.6 | async-start | bytes 4194304 | tf_op jit(solution)/shard_map/psum | solution.py:21
  523.6 4.2 copy-start.1
  530.8 1.0 copy-start.4
  534.3 80.9 %copy-start.5 = (bf16[1024,512]{1,0:T(8,128)(2,1)S(1)}, bf16[1024,512]{1,0:T(8,128)(2,1)}, u32[]{:S(2)}) copy-start(bf16[1024,512]{1,0:T(8,128)(2,1)} %copy-done.4) | copy-start | bytes 3145732
Sparse Core Ops, SparseCore 0:
  147.2 35.1 reduce-scatter.3
  231.2 35.5 all-gather.1
  450.1 73.4 all-reduce.2
  534.5 80.7 all-reduce.4
where the time goes:
time: 627 us; the launch traced here: 626 us
  blocking collectives  254 us (41%)
  waiting for transfers between devices  248 us (40%)
  local copies, waits for them, and re-layouts  47.8 us (8%)
  other arithmetic  24.9 us (4%)
  matrix products  19.6 us (3%)
  starting transfers between devices  16.4 us (3%)
  between operations  14.7 us (2%)
    all_to_all x1, blocking collectives, per_device(): lax.all_to_all(send_scaled, 'expert', split_axis=0, concat_axis=0, tiled=...  160 us
    psum x2, waiting for transfers between devices, gram_sum(): return lax.psum(partial_gram.astype(jnp.bfloat16), 'dp').astype(jnp.float32)  154 us
    all_to_all x1, blocking collectives, per_device(): lax.all_to_all(send_grad, 'expert', split_axis=0, concat_axis=0, tiled=True)  94.8 us
    all_gather x1, waiting for transfers between devices, per_device(): whole_scaled = lax.all_gather(scaled_part, 'dp', axis=2, tiled=True)  35.5 us
    unnamed x5, waiting for transfers between devices  35.4 us
    all_to_all x1, waiting for transfers between devices, per_device(): lax.all_to_all(summed.reshape(experts, capacity, -1).astype(jnp.bfloat16)...  23.1 us
    scatter x2, local copies, waits for them, and re-layouts, place_slots(): return empty_rows.at[slot_index].set(values)  20.6 us
    another operation x3, other arithmetic  18.2 us
  transfers between devices with their start and end apart: 5, of which 5 were waited for; matrix products, arithmetic and copies ran while one was open for 0% of the time, Pallas kernels for 0%

commit v1 on v0

--- a/solution.py
+++ b/solution.py
@@ -39,7 +39,8 @@
         experts, capacity, width_part
     )
     scaled_part = (gate_prob[:, :, None] * hidden.astype(jnp.float32)).astype(jnp.bfloat16)
-    whole_scaled = lax.all_gather(scaled_part, "dp", axis=2, tiled=True)
+    sent = jnp.stack([scaled_part] * lax.axis_size("dp"))
+    whole_scaled = jnp.concatenate(lax.all_to_all(sent, "dp", 0, 0), axis=2)
     send_scaled = place_slots(
         slot_index, whole_scaled.reshape(pair_count, -1), total_slots
     ).reshape(experts, capacity, -1)

time: 627 us -> 607 us (0.968)
  waiting for transfers between devices: 248 us -> 211 us
  blocking collectives: 254 us -> 277 us
    all_gather x1 -> x0, waiting for transfers between devices: 35.5 us -> none  [per_device(): whole_scaled = lax.all_gather(scaled_part, 'dp', axis=2, tiled=True)]
    all_to_all x0 -> x1, blocking collectives: none -> 31.3 us  [per_device(): whole_scaled = jnp.concatenate(lax.all_to_all(sent, 'dp', 0, 0), axis=2)]
    all_to_all x1, blocking collectives: 160 us -> 151 us  [per_device(): lax.all_to_all(send_scaled, 'expert', split_axis=0, concat_axis=0, tiled=...]
    unnamed x5 -> x4, waiting for transfers between devices: 35.4 us -> 35.3 us
  transfers between devices with their start and end apart: 5 -> 4, of which waited for: 5 -> 4; matrix products, arithmetic and copies ran while one was open for 0% -> 0% of each run, Pallas kernels for 0% -> 0%
where the time goes in v1:
time: 607 us; the launch traced here: 606 us
  blocking collectives  277 us (46%)
  waiting for transfers between devices  211 us (35%)
  local copies, waits for them, and re-layouts  44.5 us (7%)
  other arithmetic  23.8 us (4%)
  matrix products  19.6 us (3%)
  starting transfers between devices  16 us (3%)
  between operations  14.7 us (2%)
    psum x2, waiting for transfers between devices, gram_sum(): return lax.psum(partial_gram.astype(jnp.bfloat16), 'dp').astype(jnp.float32)  153 us
    all_to_all x1, blocking collectives, per_device(): lax.all_to_all(send_scaled, 'expert', split_axis=0, concat_axis=0, tiled=...  151 us
    all_to_all x1, blocking collectives, per_device(): lax.all_to_all(send_grad, 'expert', split_axis=0, concat_axis=0, tiled=True)  94.8 us
    unnamed x4, waiting for transfers between devices  35.3 us
    all_to_all x1, blocking collectives, per_device(): whole_scaled = jnp.concatenate(lax.all_to_all(sent, 'dp', 0, 0), axis=2)  31.3 us
    all_to_all x1, waiting for transfers between devices, per_device(): lax.all_to_all(summed.reshape(experts, capacity, -1).astype(jnp.bfloat16)...  23 us
    scatter x2, local copies, waits for them, and re-layouts, place_slots(): return empty_rows.at[slot_index].set(values)  19.9 us
    another operation x3, other arithmetic  18.2 us
  transfers between devices with their start and end apart: 4, of which 4 were waited for; matrix products, arithmetic and copies ran while one was open for 0% of the time, Pallas kernels for 0%

profile of v1, /device:TPU:2, one launch (start us, length us, event | category | flops | bytes accessed | tf_op | source)
XLA Modules:
  0.0 606.4 jit_solution(2028359757058308746)
XLA Ops:
  7.2 0.0 reduce-scatter.4.cloned.1.call-start
  7.2 0.8 broadcast_multiply_fusion
  8.0 0.8 copy.27
  8.8 0.2 eq.29
  9.0 0.2 eq.25
  9.2 0.1 copy.26
  9.3 0.2 mul.64
  9.6 18.0 %reduce-window.6 = s32[64,8,128]{2,1,0:T(8,128)S(1)} reduce-window(s32[64,8,128]{2,1,0:T(8,128)S(1)} %fusion.23, s32[]{:T(128)} %constant.16.clone.1), window={size=1x1x128 pad=0_0x0_0x127_0}, to_apply=%region_0.0 | reduce-window | flops 8323072 | bytes 524292 | tf_op jit(solution)/shard_map/reduce-window
  27.6 0.1 slice.12
  27.7 0.1 copy.29
  27.9 0.1 copy.30
  28.0 0.1 broadcast_add_fusion
  28.1 0.1 fusion.22
  28.2 12.8 %scatter_custom_fusion = bf16[1280,512]{1,0:T(8,128)(2,1)S(1)} fusion(s32[1024]{0:T(1024)S(1)} %bitcast.54, bf16[512,512]{1,0:T(8,128)(2,1)} %param.5, s32[1024]{0:T(1024)S(1)} %broadcast_clamp_fusion.1, bf16[]{:T(256)} %constant.13.clone.1), kind=kCustom, calls=%fused_computation.24 | custom fusion | bytes 1311232 | tf_op jit(solution)/shard_map/scatter | solution.py:26
  41.0 1.3 reshape.126
  42.3 94.8 %all_to_all.20 = bf16[64,20,512]{2,1,0:T(8,128)(2,1)S(1)} all-to-all(bf16[64,20,512]{2,1,0:T(8,128)(2,1)} %reshape.126), channel_id=1, replica_groups=mesh['dp'=8,'expert'=64] {'expert'}, dimensions={0} | all-to-all | bytes 2621440 | tf_op jit(solution)/shard_map/all_to_all | solution.py:48
  137.1 1.3 reshape.127
  138.4 4.4 convolution_convert_fusion
  142.8 4.4 copy.34
  147.2 0.0 reduce-scatter.4.cloned.1.call-update
  147.2 35.3 %reduce-scatter.4.cloned.1.call-done = bf16[128,1280]{1,0:T(8,128)(2,1)} async-done(((bf16[1024,1280]{1,0:T(8,128)(2,1)}), bf16[128,1280]{1,0:T(8,128)(2,1)}) %reduce-scatter.4.cloned.1.call-update) | async-done | bytes 327696
  182.5 1.2 copy.35
  183.7 0.8 convert_element_type.61
  184.5 15.7 %all-to-all-start.1 = ((bf16[64,20,128]{2,1,0:T(8,128)(2,1)}), bf16[64,20,128]{2,1,0:T(8,128)(2,1)S(1)}, u32[]{:S(2)}, u32[]{:S(2)}) async-start(bf16[64,20,128]{2,1,0:T(8,128)(2,1)} %convert_element_type.61), calls=%async_computation.1 | async-start | bytes 786432 | tf_op jit(solution)/shard_map/all_to_all | solution.py:64
  200.2 0.2 all-reduce.3.cloned.1.call-start
  200.4 0.1 copy.25
  200.6 23.0 %all-to-all-done.1 = bf16[64,20,128]{2,1,0:T(8,128)(2,1)S(1)} async-done(((bf16[64,20,128]{2,1,0:T(8,128)(2,1)}), bf16[64,20,128]{2,1,0:T(8,128)(2,1)S(1)}, u32[]{:S(2)}, u32[]{:S(2)}) %all-to-all-start.1) | async-done | bytes 327712 | tf_op jit(solution)/shard_map/all_to_all | solution.py:64
  223.6 0.1 reshape.133
  223.7 2.8 gather_fusion
  226.5 1.4 multiply_convert_fusion.2
  227.9 1.1 stack.2
  229.0 31.3 %all_to_all.21 = bf16[8,512,2,128]{3,2,1,0:T(2,128)(2,1)S(1)} all-to-all(bf16[8,512,2,128]{3,2,1,0:T(2,128)(2,1)S(1)} %stack.2), channel_id=1, replica_groups=mesh['dp'=8,'expert'=64] {'dp'}, dimensions={0} | all-to-all | bytes 4194304 | tf_op jit(solution)/shard_map/all_to_all | solution.py:43
  260.3 2.4 copy.31
  262.7 7.2 %scatter_custom_fusion.1 = bf16[1280,1024]{1,0:T(8,128)(2,1)} fusion(s32[1024]{0:T(1024)S(1)} %bitcast.56, bf16[128,8,8,128]{3,2,1,0:T(8,128)(2,1)S(1)} %bitcast.47, bf16[]{:T(256)} %constant.13.clone.1), kind=kCustom, calls=%fused_computation.11 | custom fusion | bytes 4718594 | tf_op jit(solution)/shard_map/scatter | solution.py:26
  269.9 5.2 reshape.131
  275.1 150.6 %all_to_all.22 = bf16[64,20,1024]{2,1,0:T(8,128)(2,1)S(1)} all-to-all(bf16[64,20,1024]{2,1,0:T(8,128)(2,1)} %reshape.131), channel_id=1, replica_groups=mesh['dp'=8,'expert'=64] {'expert'}, dimensions={0} | all-to-all | bytes 5242880 | tf_op jit(solution)/shard_map/all_to_all | solution.py:49
  425.7 2.9 bitcast_convert_fusion
  428.6 1.0 copy-done.6
  429.5 2.6 convolution_convert_fusion.2
  432.1 0.0 all-reduce.3.cloned.1.call-update
  432.2 0.0 all-reduce.5.cloned.1.call-start
  432.2 71.9 %all-reduce.3.cloned.1.call-done = bf16[1024,1024]{1,0:T(8,128)(2,1)} async-done(((bf16[1024,1024]{1,0:T(8,128)(2,1)}), bf16[1024,1024]{1,0:T(8,128)(2,1)}) %all-reduce.3.cloned.1.call-update) | async-done | bytes 2097168 | tf_op jit(solution)/shard_map/psum | solution.py:21
  504.1 3.4 fusion
  508.2 2.9 subtract_convert_fusion
  511.2 1.0 copy-done.7
  512.2 2.6 convolution_convert_fusion.1
  514.8 80.9 %all-reduce.5.cloned.1.call-done = bf16[1024,1024]{1,0:T(8,128)(2,1)} async-done(((bf16[1024,1024]{1,0:T(8,128)(2,1)}), bf16[1024,1024]{1,0:T(8,128)(2,1)}) %all-reduce.5.cloned.1.call-update) | async-done | bytes 2097168 | tf_op jit(solution)/shard_map/psum | solution.py:21
  595.7 4.2 multiply_bitcast_fusion
  (24 shorter events, 0.1 us)
Async XLA Ops:
  7.2 131.2 %copy-start = (bf16[1,1024,512]{2,1,0:T(8,128)(2,1)S(1)}, bf16[1,1024,512]{2,1,0:T(8,128)(2,1)}, u32[]{:S(2)}) copy-start(bf16[1,1024,512]{2,1,0:T(8,128)(2,1)} %param.9) | copy-start | bytes 3145732
  7.2 175.3 %reduce-scatter.4.cloned.1.call-start = ((), (), s32[]{:S(2)}) async-start(), calls=%async_computation.7 | async-start | bytes 2949120
  137.1 5.7 copy-start.1
  147.2 53.2 %copy-start.5 = (f32[512,2]{0,1:T(2,128)S(1)}, f32[512,2]{0,1:T(2,128)}, u32[]{:S(2)}) copy-start(f32[512,2]{0,1:T(2,128)} %param.7) | copy-start | bytes 12292
  184.5 39.1 %all-to-all-start.1 = ((bf16[64,20,128]{2,1,0:T(8,128)(2,1)}), bf16[64,20,128]{2,1,0:T(8,128)(2,1)S(1)}, u32[]{:S(2)}, u32[]{:S(2)}) async-start(bf16[64,20,128]{2,1,0:T(8,128)(2,1)} %convert_element_type.61), calls=%async_computation.1 | async-start | bytes 786432 | tf_op jit(solution)/shard_map/all_to_all | solution.py:64
  200.2 303.9 %all-reduce.3.cloned.1.call-start = ((), (), s32[]{:S(2)}) async-start(), calls=%async_computation.5 | async-start | bytes 4194304 | tf_op jit(solution)/shard_map/psum | solution.py:21
  223.7 2.8 copy-start.4
  275.1 150.6 %copy-start.2 = (bf16[64,20,512]{2,1,0:T(8,128)(2,1)S(1)}, bf16[64,20,512]{2,1,0:T(8,128)(2,1)}, u32[]{:S(2)}) copy-start(bf16[64,20,512]{2,1,0:T(8,128)(2,1)} %copy-done.1) | copy-start | bytes 3932164
  428.6 1.0 copy-start.6
  432.2 163.5 %all-reduce.5.cloned.1.call-start = ((), (), s32[]{:S(2)}) async-start(), calls=%async_computation.6 | async-start | bytes 4194304 | tf_op jit(solution)/shard_map/psum | solution.py:21
  504.1 4.2 copy-start.3
  511.2 1.0 copy-start.7
  514.8 80.9 %copy-start.8 = (bf16[1024,512]{1,0:T(8,128)(2,1)S(1)}, bf16[1024,512]{1,0:T(8,128)(2,1)}, u32[]{:S(2)}) copy-start(bf16[1024,512]{1,0:T(8,128)(2,1)} %copy-done.7) | copy-start | bytes 3145732
Sparse Core Ops, SparseCore 0:
  147.3 35.1 reduce-scatter.3
  432.3 71.7 all-reduce.2
  514.9 80.6 all-reduce.4
